TPU v7x, 32 devices: a whole 2x2x4 slice. The times are simulated.
32 devices in a mesh: shot: 2 (over x), tile: 16 (over z, y, core).
Axes of the slice: x: 2, y: 2, z: 4, core: 2. Of those that a mesh axis runs over, the one named last changes fastest.
Arguments:
- wave_now: float32 [4, 32, 32, 128], P('shot', 'tile'), parts along dimension 0, may hold values from -6 to 6
- wave_prev: float32 [4, 32, 32, 128], P('shot', 'tile'), parts along dimension 0, may hold values from -6 to 6
- facies: int32 [32, 32, 128], P('tile'), may hold values from 0 to 7
- velocity_table: float32 [8], replicated, may hold values from 0.05 to 0.2
- epsilon_table: float32 [8], replicated, may hold values from 0 to 0.2
- tilt_table: float32 [8], replicated, may hold values from -0.6 to 0.6
- source_cell: int32 [2], P('shot'), parts along dimension 0, may hold values from 0 to 4095
- source_wavelet: float32 [8], P('shot'), parts along dimension 0, may hold values from -8 to 8
- receiver_cells: int32 [4096], P('shot'), parts along dimension 0, may hold values from 0 to 4095
- receiver_data: float32 [4, 4096], P(None, 'shot'), parts along dimension 1, may hold values from -6 to 6
Outputs:
- filtered: bfloat16 [64, 32, 32, 128], P('shot', None, 'tile'), parts along dimension 0
- wave_out: float32 [4, 32, 32, 128], P('shot', 'tile'), parts along dimension 0
There are 2 independent parts, one for each index of `shot`. A program takes and returns all parts, laid end to end along the dimension named above; an argument that names none is the same for every part. Nothing has to cross between parts.
Inputs may be any that keep to these rules, and one draw needn't show every extreme that they name: `source_cell`: a surface cell y * 128 + x. `receiver_cells`: surface cells y * 128 + x; cells may repeat.
All inputs are finite; a program needn't handle non-finite values.
Results may differ from a plain program's by a relative error of at most 0.001.
The roundings to bfloat16 on the way count: a program that leaves them out, or rounds other values in their place, can miss the bound.
Values may be sent and summed in bfloat16 or wider, within the bound.
A program may use at most 64 MiB of HBM per device.

v0:
```python
import jax
import jax.numpy as jnp
from jax import lax
from jax.sharding import PartitionSpec as P

NLAG = 32
STEPS = 4


def extended_2(value, sides, width):
    for axis, dim in sides:
        size, length = (lax.axis_size(axis), value.shape[dim])
        up = [(i, (i + 1) % size) for i in range(size - 1)]
        down = [(j, i) for i, j in up]
        last = lax.slice_in_dim(value, length - width, length, axis=dim)
        leading = lax.slice_in_dim(value, 0, width, axis=dim)
        before = lax.ppermute(last, axis, up)
        after = lax.ppermute(leading, axis, down)
        value = jnp.concatenate([before, value, after], axis=dim)
    return value


def wave_update(padded, previous, velocity, aniso, tilt):
    center = padded[:, 1:-1, 1:-1, 1:-1]
    along_x = padded[:, 1:-1, 1:-1, 2:] + padded[:, 1:-1, 1:-1, :-2] - 2.0 * center
    along_y = padded[:, 2:, 1:-1, 1:-1] + padded[:, :-2, 1:-1, 1:-1] - 2.0 * center
    along_z = padded[:, 1:-1, 2:, 1:-1] + padded[:, 1:-1, :-2, 1:-1] - 2.0 * center
    mixed = (
        padded[:, 1:-1, 2:, 2:]
        - padded[:, 1:-1, :-2, 2:]
        - padded[:, 1:-1, 2:, :-2]
        + padded[:, 1:-1, :-2, :-2]
    )
    operator = aniso * (along_x + along_y) + along_z + 0.25 * tilt * mixed
    return 2.0 * center - previous + velocity * operator


def filter_planes(extended):
    values = extended.astype(jnp.float32)
    spec = [(0, 0)] * (values.ndim - 3) + [(1, 1), (0, 0), (1, 1)]
    padded = jnp.pad(values, spec)
    center = padded[..., 1:-1, 1:-1, 1:-1]
    neighbours = padded[..., 2:, 1:-1, 1:-1] + padded[..., :-2, 1:-1, 1:-1]
    neighbours = neighbours + padded[..., 1:-1, 2:, 1:-1] + padded[..., 1:-1, :-2, 1:-1]
    neighbours = neighbours + padded[..., 1:-1, 1:-1, 2:] + padded[..., 1:-1, 1:-1, :-2]
    return (0.125 * (6.0 * center - neighbours)).astype(jnp.bfloat16)


def lookup(facies, table):
    result = jnp.zeros(facies.shape, jnp.float32)
    for facies_id in range(table.shape[0]):
        result = jnp.where(facies == facies_id, table[facies_id], result)
    return result


def surface_term(cells, values, first_cell, count):
    local_cell = cells - first_cell
    inside = (local_cell >= 0) & (local_cell < count)
    target = jnp.where(inside, local_cell, count)
    return jnp.zeros((count + 1,), jnp.float32).at[target].add(values)[:count]


def correlate(snapshot_pair, margin):
    columns = snapshot_pair.shape[-1]
    source_padded = jnp.pad(
        snapshot_pair[0].astype(jnp.float32), ((0, 0), (0, 0), (margin, margin))
    )
    receiver_padded = jnp.pad(
        snapshot_pair[1].astype(jnp.float32), ((0, 0), (0, 0), (margin, margin))
    )
    return jnp.stack(
        [
            source_padded[:, :, margin - offset : margin - offset + columns]
            * receiver_padded[:, :, margin + offset : margin + offset + columns]
            for offset in range(-margin, margin)
        ]
    )


def shards(
    wave_now,
    wave_prev,
    facies,
    velocity_table,
    epsilon_table,
    tilt_table,
    source_cell,
    source_wavelet,
    receiver_cells,
    receiver_data,
):
    tile_rows, depth_planes, columns = facies.shape
    tile_count = lax.axis_size("tile")
    velocity = lookup(facies, velocity_table)
    aniso = 1.0 + 2.0 * lookup(facies, epsilon_table)
    tilt = lookup(facies, tilt_table)
    first_cell = lax.axis_index("tile") * (tile_rows * columns)
    surface_count = tile_rows * columns
    margin = NLAG // 2
    extra = 2
    image_sum = jnp.zeros(
        (NLAG, tile_rows * tile_count, depth_planes // tile_count + extra, columns), jnp.float32
    )
    current, previous = (wave_now, wave_prev)
    for step in range(STEPS):
        padded = extended_2(current, (("tile", 1),), 1)
        padded = jnp.pad(padded, ((0, 0), (0, 0), (1, 1), (1, 1)))
        advanced = wave_update(padded, previous, velocity, aniso, tilt)
        source_plane = surface_term(
            source_cell,
            jnp.broadcast_to(source_wavelet[step], source_cell.shape),
            first_cell,
            surface_count,
        )
        receiver_plane = surface_term(
            receiver_cells, receiver_data[step], first_cell, surface_count
        )
        surface = jnp.stack([source_plane, receiver_plane]).reshape(2, tile_rows, columns)
        advanced = advanced.at[:, :, 0, :].add(surface)
        previous, current = (current, advanced)
        if step % 2 == 1:
            moved = lax.all_to_all(
                current.astype(jnp.bfloat16), "tile", split_axis=2, concat_axis=1, tiled=True
            )
            moved = extended_2(moved, (("tile", 2),), 1)
            image_sum = image_sum + correlate(moved, margin)
    image = image_sum.astype(jnp.bfloat16)
    grouped = image.reshape((NLAG // 8, 8) + image.shape[1:])
    filtered = lax.map(filter_planes, grouped)
    filtered = filtered.reshape((NLAG, image.shape[1], image.shape[2] - 2, image.shape[3]))
    return (filtered, current)


def solution(mesh):
    return jax.shard_map(
        shards,
        mesh=mesh,
        in_specs=(
            P("shot", "tile", None, None),
            P("shot", "tile", None, None),
            P("tile", None, None),
            P(),
            P(),
            P(),
            P("shot"),
            P("shot"),
            P("shot"),
            P(None, "shot"),
        ),
        out_specs=(P("shot", None, "tile", None), P("shot", "tile", None, None)),
        check_vma=False,
    )
```

profile of v0, /device:TPU:8, one launch (start us, length us, event | category | flops | bytes accessed | tf_op | source)
XLA Modules:
  0.0 171.2 jit_solution(15353651140003492565)
XLA Ops:
  0.7 0.8 fusion.127
  1.5 1.9 %collective-permute-start = (f32[2,1,32,128]{3,1,0,2:T(1,128)S(1)}, f32[2,1,32,128]{3,1,0,2:T(1,128)S(1)}, u32[]{:S(2)}, u32[]{:S(2)}) collective-permute-start(f32[2,1,32,128]{3,1,0,2:T(1,128)S(1)} %copy.69), channel_id=1, source_target_pairs={{0,1},{1,2},{2,3},{3,4},{4,5},{5,6},{6,7},{7,8},{8,9},{9,10},{10,1... | collective-permute-start | bytes 98312 | tf_op jit(solution)/shard_map/ppermute | solution.py:17
  3.5 4.5 %collective-permute-start.1 = (f32[2,1,32,128]{3,1,0,2:T(1,128)S(1)}, f32[2,1,32,128]{3,1,0,2:T(1,128)S(1)}, u32[]{:S(2)}, u32[]{:S(2)}) collective-permute-start(f32[2,1,32,128]{3,1,0,2:T(1,128)S(1)} %copy.70), channel_id=1, source_target_pairs={{1,0},{2,1},{3,2},{4,3},{5,4},{6,5},{7,6},{8,7},{9,8},{10,9},{11,1... | collective-permute-start | bytes 98312 | tf_op jit(solution)/shard_map/ppermute | solution.py:18
  8.0 1.6 fusion.133
  9.7 1.6 fusion.131
  11.3 1.6 fusion.132
  13.6 0.9 fusion.129
  14.5 0.7 compare_select_fusion
  15.8 2.0 %select_dynamic-update-slice_fusion.3 = f32[257]{0:T(512)S(1)} fusion(f32[257]{0:T(512)S(1)} %broadcast.196.clone, s32[]{:T(128)} %bitcast.28, f32[4]{0:T(128)} %param.35, s32[1]{0:T(128)} %compare_select_fusion.1), kind=kLoop, calls=%fused_computation.348 | loop fusion | flops 4 | bytes 524 | tf_op jit(solution)/shard_map/scatter-add | solution.py:60
  17.8 2.1 %select_dynamic-update-slice_fusion.2 = f32[257]{0:T(512)S(1)} fusion(f32[257]{0:T(512)S(1)} %broadcast.196.clone.1, s32[]{:T(128)} %bitcast.28, f32[4]{0:T(128)} %param.35, s32[1]{0:T(128)} %compare_select_fusion.1), kind=kLoop, calls=%fused_computation.347 | loop fusion | flops 4 | bytes 524 | tf_op jit(solution)/shard_map/scatter-add | solution.py:60
  19.9 14.7 %scatter_custom_fusion = f32[257]{0:T(512)S(1)} fusion(s32[2048]{0:T(1024)S(1)} %compare_select_fusion, f32[2048]{0:T(1024)S(1)} %bitcast.333, f32[]{:T(128)} %constant.226.clone.1), kind=kCustom, calls=%fused_computation.343 | custom fusion | flops 2048 | bytes 1032 | tf_op jit(solution)/shard_map/scatter-add | solution.py:60
  34.6 14.7 %scatter_custom_fusion.1 = f32[257]{0:T(512)S(1)} fusion(s32[2048]{0:T(1024)S(1)} %compare_select_fusion, f32[2048]{0:T(1024)S(1)} %bitcast.332, f32[]{:T(128)} %constant.226.clone.1), kind=kCustom, calls=%fused_computation.341 | custom fusion | flops 2048 | bytes 1032 | tf_op jit(solution)/shard_map/scatter-add | solution.py:60
  49.2 6.0 %select_select_fusion = (f32[2,32,128]{2,1,0:T(8,128)S(1)}, pred[2,32,128]{2,1,0:T(8,128)(4,1)S(1)}, pred[2,32,128]{2,1,0:T(8,128)(4,1)S(1)}, pred[2,32,128]{2,1...) fusion(f32[]{:T(128)} %bitcast.10, f32[]{:T(128)} %bitcast.9, ...), kind=kLoop, calls=%fused_computation.304 | loop fusion | flops 131072 | bytes 131104 | tf_op jit(solution)/shard_map/jit(_where)/select_n | solution.py:52
  55.2 4.9 %multiply_add_fusion = f32[2,32,128]{2,1,0:T(8,128)S(1)} fusion(pred[2,32,128]{2,1,0:T(8,128)(4,1)S(1)} %get-tuple-element.172, pred[2,32,128]{2,1,0:T(8,128)(4,1)S(1)} %get-tuple-element.171, pred[2,32,128]{2,1,0:T(8,128)(4,1)S(1)} %get-tuple-element.170, pred[2,32,128]{2,1,0:T(8,128)(4,1)S(1)} %get-tuple-element.169, ...), kind=kLoop, calls=%fused_computation.303 | loop fusion | flops 81920 | bytes 98336 | tf_op jit(solution)/shard_map/add | solution.py:95
  60.2 5.0 %select_multiply_fusion = f32[2,32,128]{2,1,0:T(8,128)S(1)} fusion(pred[2,32,128]{2,1,0:T(8,128)(4,1)S(1)} %get-tuple-element.172, pred[2,32,128]{2,1,0:T(8,128)(4,1)S(1)} %get-tuple-element.171, pred[2,32,128]{2,1,0:T(8,128)(4,1)S(1)} %get-tuple-element.170, pred[2,32,128]{2,1,0:T(8,128)(4,1)S(1)} %get-tuple-element.169, ...), kind=kLoop, calls=%fused_computation.302 | loop fusion | flops 73728 | bytes 98336 | tf_op jit(solution)/shard_map/mul | solution.py:34
  65.2 2.1 %select_dynamic-update-slice_fusion.1 = f32[257]{0:T(512)S(1)} fusion(f32[257]{0:T(512)S(1)} %broadcast.196.clone.2, s32[]{:T(128)} %bitcast.28, f32[4]{0:T(128)} %param.35, s32[1]{0:T(128)} %compare_select_fusion.1), kind=kLoop, calls=%fused_computation.346 | loop fusion | flops 4 | bytes 524 | tf_op jit(solution)/shard_map/scatter-add | solution.py:60
  67.2 0.9 copy.65
  68.2 14.7 %scatter_custom_fusion.2 = f32[257]{0:T(512)S(1)} fusion(s32[2048]{0:T(1024)S(1)} %compare_select_fusion, f32[2048]{0:T(1024)S(1)} %bitcast.331, f32[]{:T(128)} %constant.226.clone.1), kind=kCustom, calls=%fused_computation.339 | custom fusion | flops 2048 | bytes 1032 | tf_op jit(solution)/shard_map/scatter-add | solution.py:60
  82.9 0.5 select_maximum_fusion.6
  83.4 1.3 fusion.105
  84.8 1.9 %collective-permute-start.2 = (f32[2,1,32,128]{3,1,0,2:T(1,128)S(1)}, f32[2,1,32,128]{3,1,0,2:T(1,128)S(1)}, u32[]{:S(2)}, u32[]{:S(2)}) collective-permute-start(f32[2,1,32,128]{3,1,0,2:T(1,128)S(1)} %get-tuple-element.183), channel_id=1, source_target_pairs={{0,1},{1,2},{2,3},{3,4},{4,5},{5,6},{6,7},{7,8},{8,9},{9,10},{10,1... | collective-permute-start | bytes 98312 | tf_op jit(solution)/shard_map/ppermute | solution.py:17
  86.7 4.5 %collective-permute-start.3 = (f32[2,1,32,128]{3,1,0,2:T(1,128)S(1)}, f32[2,1,32,128]{3,1,0,2:T(1,128)S(1)}, u32[]{:S(2)}, u32[]{:S(2)}) collective-permute-start(f32[2,1,32,128]{3,1,0,2:T(1,128)S(1)} %get-tuple-element.184), channel_id=1, source_target_pairs={{1,0},{2,1},{3,2},{4,3},{5,4},{6,5},{7,6},{8,7},{9,8},{10,9},{11,1... | collective-permute-start | bytes 98312 | tf_op jit(solution)/shard_map/ppermute | solution.py:18
  91.3 1.6 collective-permute-done.3
  92.8 0.5 select_maximum_fusion.4
  93.3 0.5 fusion.95
  93.9 1.9 %collective-permute-start.6 = (f32[2,1,32,128]{3,1,0,2:T(1,128)S(1)}, f32[2,1,32,128]{3,1,0,2:T(1,128)S(1)}, u32[]{:S(2)}, u32[]{:S(2)}) collective-permute-start(f32[2,1,32,128]{3,1,0,2:T(1,128)S(1)} %get-tuple-element.179), channel_id=1, source_target_pairs={{0,1},{1,2},{2,3},{3,4},{4,5},{5,6},{6,7},{7,8},{8,9},{9,10},{10,1... | collective-permute-start | bytes 98312 | tf_op jit(solution)/shard_map/ppermute | solution.py:17
  95.8 4.5 %collective-permute-start.7 = (f32[2,1,32,128]{3,1,0,2:T(1,128)S(1)}, f32[2,1,32,128]{3,1,0,2:T(1,128)S(1)}, u32[]{:S(2)}, u32[]{:S(2)}) collective-permute-start(f32[2,1,32,128]{3,1,0,2:T(1,128)S(1)} %get-tuple-element.180), channel_id=1, source_target_pairs={{1,0},{2,1},{3,2},{4,3},{5,4},{6,5},{7,6},{8,7},{9,8},{10,9},{11,1... | collective-permute-start | bytes 98312 | tf_op jit(solution)/shard_map/ppermute | solution.py:18
  100.4 1.4 select_dynamic-update-slice_fusion
  101.8 14.7 %scatter_custom_fusion.3 = f32[257]{0:T(512)S(1)} fusion(s32[2048]{0:T(1024)S(1)} %compare_select_fusion, f32[2048]{0:T(1024)S(1)} %bitcast.330, f32[]{:T(128)} %constant.226.clone.1), kind=kCustom, calls=%fused_computation.337 | custom fusion | flops 2048 | bytes 1032 | tf_op jit(solution)/shard_map/scatter-add | solution.py:60
  116.5 0.5 select_maximum_fusion.2
  117.0 0.5 fusion.54
  117.5 1.9 %collective-permute-start.8 = (f32[2,1,32,128]{3,1,0,2:T(1,128)S(1)}, f32[2,1,32,128]{3,1,0,2:T(1,128)S(1)}, u32[]{:S(2)}, u32[]{:S(2)}) collective-permute-start(f32[2,1,32,128]{3,1,0,2:T(1,128)S(1)} %get-tuple-element.177), channel_id=1, source_target_pairs={{0,1},{1,2},{2,3},{3,4},{4,5},{5,6},{6,7},{7,8},{8,9},{9,10},{10,1... | collective-permute-start | bytes 98312 | tf_op jit(solution)/shard_map/ppermute | solution.py:17
  119.4 4.5 %collective-permute-start.9 = (f32[2,1,32,128]{3,1,0,2:T(1,128)S(1)}, f32[2,1,32,128]{3,1,0,2:T(1,128)S(1)}, u32[]{:S(2)}, u32[]{:S(2)}) collective-permute-start(f32[2,1,32,128]{3,1,0,2:T(1,128)S(1)} %get-tuple-element.178), channel_id=1, source_target_pairs={{1,0},{2,1},{3,2},{4,3},{5,4},{6,5},{7,6},{8,7},{9,8},{10,9},{11,1... | collective-permute-start | bytes 98312 | tf_op jit(solution)/shard_map/ppermute | solution.py:18
  124.0 1.6 collective-permute-done.9
  125.6 0.5 select_maximum_fusion
  126.0 1.0 fusion.44
  127.0 0.6 convert_element_type.75
  127.6 6.5 %all-to-all-start.1 = ((bf16[2,2,32,128]{3,1,0,2:T(2,128)(2,1)}), bf16[2,2,32,128]{3,1,0,2:T(2,128)(2,1)S(1)}, u32[]{:S(2)}, u32[]{:S(2)}) async-start(bf16[2,2,32,128]{3,1,0,2:T(2,128)(2,1)} %convert_element_type.75), calls=%async_computation.1 | async-start | bytes 65536 | tf_op jit(solution)/shard_map/all_to_all | solution.py:122
  134.2 0.6 copy.79
  134.8 4.4 %all-to-all-done.1 = bf16[2,2,32,128]{3,1,0,2:T(2,128)(2,1)S(1)} async-done(((bf16[2,2,32,128]{3,1,0,2:T(2,128)(2,1)}), bf16[2,2,32,128]{3,1,0,2:T(2,128)(2,1)S(1)}, u32[]{:S(2)}, u32[]{:S(2)}) %all-to-all-start.1) | async-done | bytes 32800 | tf_op jit(solution)/shard_map/all_to_all | solution.py:122
  139.2 5.0 %all-to-all-start = ((bf16[2,2,32,128]{3,1,0,2:T(2,128)(2,1)}), bf16[2,2,32,128]{3,1,0,2:T(2,128)(2,1)S(1)}, u32[]{:S(2)}, u32[]{:S(2)}) async-start(bf16[2,2,32,128]{3,1,0,2:T(2,128)(2,1)} %get-tuple-element.176), calls=%async_computation | async-start | bytes 65536 | tf_op jit(solution)/shard_map/all_to_all | solution.py:122
  144.2 2.0 %collective-permute-start.10 = (bf16[2,32,1,128]{3,1,2,0:T(8,128)(2,1)S(1)}, bf16[2,32,1,128]{3,1,2,0:T(8,128)(2,1)S(1)}, u32[]{:S(2)}, u32[]{:S(2)}) collective-permute-start(bf16[2,32,1,128]{3,1,2,0:T(8,128)(2,1)S(1)} %get-tuple-element.187), channel_id=1, source_target_pairs={{0,1},{1,2},{2,3},{3,4},{4,5},{5,6},{6,7},{7,8},{8,9},{9,10},{10,1... | collective-permute-start | bytes 49160 | tf_op jit(solution)/shard_map/ppermute | solution.py:17
  146.3 4.4 %collective-permute-start.11 = (bf16[2,32,1,128]{3,1,2,0:T(8,128)(2,1)S(1)}, bf16[2,32,1,128]{3,1,2,0:T(8,128)(2,1)S(1)}, u32[]{:S(2)}, u32[]{:S(2)}) collective-permute-start(bf16[2,32,1,128]{3,1,2,0:T(8,128)(2,1)S(1)} %get-tuple-element.188), channel_id=1, source_target_pairs={{1,0},{2,1},{3,2},{4,3},{5,4},{6,5},{7,6},{8,7},{9,8},{10,9},{11,1... | collective-permute-start | bytes 49160 | tf_op jit(solution)/shard_map/ppermute | solution.py:18
  150.8 1.9 %collective-permute-start.4 = (bf16[2,32,1,128]{3,1,2,0:T(8,128)(2,1)S(1)}, bf16[2,32,1,128]{3,1,2,0:T(8,128)(2,1)S(1)}, u32[]{:S(2)}, u32[]{:S(2)}) collective-permute-start(bf16[2,32,1,128]{3,1,2,0:T(8,128)(2,1)S(1)} %get-tuple-element.193), channel_id=1, source_target_pairs={{0,1},{1,2},{2,3},{3,4},{4,5},{5,6},{6,7},{7,8},{8,9},{9,10},{10,1... | collective-permute-start | bytes 49160 | tf_op jit(solution)/shard_map/ppermute | solution.py:17
  152.7 4.7 %collective-permute-start.5 = (bf16[2,32,1,128]{3,1,2,0:T(8,128)(2,1)S(1)}, bf16[2,32,1,128]{3,1,2,0:T(8,128)(2,1)S(1)}, u32[]{:S(2)}, u32[]{:S(2)}) collective-permute-start(bf16[2,32,1,128]{3,1,2,0:T(8,128)(2,1)S(1)} %get-tuple-element.194), channel_id=1, source_target_pairs={{1,0},{2,1},{3,2},{4,3},{5,4},{6,5},{7,6},{8,7},{9,8},{10,9},{11,1... | collective-permute-start | bytes 49160 | tf_op jit(solution)/shard_map/ppermute | solution.py:18
  157.8 0.1 constant_dynamic-update-slice_fusion.62
  158.0 0.1 constant_dynamic-update-slice_fusion.60
  158.2 0.1 constant_dynamic-update-slice_fusion.58
  158.3 0.1 constant_dynamic-update-slice_fusion.57
  158.4 0.1 constant_dynamic-update-slice_fusion.56
  158.5 0.1 constant_dynamic-update-slice_fusion.55
  158.6 0.1 constant_dynamic-update-slice_fusion.54
  158.7 0.1 constant_dynamic-update-slice_fusion.53
  158.8 0.1 constant_dynamic-update-slice_fusion.52
  164.5 0.5 add_convert_fusion
  165.0 6.3 %while.20 = (s32[]{:T(128)}, bf16[4,8,32,2,128]{4,3,2,1,0:T(2,128)(2,1)}, bf16[4,8,32,4,128]{4,2,3,1,0:T(8,128)(2,1)S(1)}, s32[]{:T(128)}) while((s32[]{:T(128)}, bf16[4,8,32,2,128]{4,3,2,1,0:T(2,128)(2,1)}, bf16[4,8,32,4,128]{4,2,3,1,0:T(8,128)(2,1)S(1)}, s32[]{:T(128)}) %tuple.117), condition=%wide.region_5.6_spmd, body=%wide.region_4.5_spmd.sunk | while | flops 720898 | bytes 2753081 | solution.py:129
  165.0 0.1 fusion.135
  165.2 1.4 bitcast_dynamic-update-slice_fusion.2
  166.6 0.1 fusion.135
  166.7 1.4 bitcast_dynamic-update-slice_fusion.2
  168.2 0.1 fusion.135
  168.3 1.4 bitcast_dynamic-update-slice_fusion.2
  169.7 0.1 fusion.135
  169.9 1.4 bitcast_dynamic-update-slice_fusion.2
  (107 shorter events, 6.1 us)
Async XLA Ops:
  0.6 92.7 %copy-start = (f32[2,2,32,128]{3,2,1,0:T(8,128)S(1)}, f32[2,2,32,128]{3,2,1,0:T(8,128)}, u32[]{:S(2)}) copy-start(f32[2,2,32,128]{3,2,1,0:T(8,128)} %param.28) | copy-start | bytes 196612
  0.6 99.7 %copy-start.1 = (f32[4]{0:T(128)S(1)}, f32[4]{0:T(128)}, u32[]{:S(2)}) copy-start(f32[4]{0:T(128)} %param.35) | copy-start | bytes 52
  1.5 81.4 %collective-permute-start = (f32[2,1,32,128]{3,1,0,2:T(1,128)S(1)}, f32[2,1,32,128]{3,1,0,2:T(1,128)S(1)}, u32[]{:S(2)}, u32[]{:S(2)}) collective-permute-start(f32[2,1,32,128]{3,1,0,2:T(1,128)S(1)} %copy.69), channel_id=1, source_target_pairs={{0,1},{1,2},{2,3},{3,4},{4,5},{5,6},{6,7},{7,8},{8,9},{9,10},{10,1... | collective-permute-start | bytes 98312 | tf_op jit(solution)/shard_map/ppermute | solution.py:17
  3.5 79.5 %collective-permute-start.1 = (f32[2,1,32,128]{3,1,0,2:T(1,128)S(1)}, f32[2,1,32,128]{3,1,0,2:T(1,128)S(1)}, u32[]{:S(2)}, u32[]{:S(2)}) collective-permute-start(f32[2,1,32,128]{3,1,0,2:T(1,128)S(1)} %copy.70), channel_id=1, source_target_pairs={{1,0},{2,1},{3,2},{4,3},{5,4},{6,5},{7,6},{8,7},{9,8},{10,9},{11,1... | collective-permute-start | bytes 98312 | tf_op jit(solution)/shard_map/ppermute | solution.py:18
  84.8 6.5 %collective-permute-start.2 = (f32[2,1,32,128]{3,1,0,2:T(1,128)S(1)}, f32[2,1,32,128]{3,1,0,2:T(1,128)S(1)}, u32[]{:S(2)}, u32[]{:S(2)}) collective-permute-start(f32[2,1,32,128]{3,1,0,2:T(1,128)S(1)} %get-tuple-element.183), channel_id=1, source_target_pairs={{0,1},{1,2},{2,3},{3,4},{4,5},{5,6},{6,7},{7,8},{8,9},{9,10},{10,1... | collective-permute-start | bytes 98312 | tf_op jit(solution)/shard_map/ppermute | solution.py:17
  86.7 6.1 %collective-permute-start.3 = (f32[2,1,32,128]{3,1,0,2:T(1,128)S(1)}, f32[2,1,32,128]{3,1,0,2:T(1,128)S(1)}, u32[]{:S(2)}, u32[]{:S(2)}) collective-permute-start(f32[2,1,32,128]{3,1,0,2:T(1,128)S(1)} %get-tuple-element.184), channel_id=1, source_target_pairs={{1,0},{2,1},{3,2},{4,3},{5,4},{6,5},{7,6},{8,7},{9,8},{10,9},{11,1... | collective-permute-start | bytes 98312 | tf_op jit(solution)/shard_map/ppermute | solution.py:18
  93.9 22.6 %collective-permute-start.6 = (f32[2,1,32,128]{3,1,0,2:T(1,128)S(1)}, f32[2,1,32,128]{3,1,0,2:T(1,128)S(1)}, u32[]{:S(2)}, u32[]{:S(2)}) collective-permute-start(f32[2,1,32,128]{3,1,0,2:T(1,128)S(1)} %get-tuple-element.179), channel_id=1, source_target_pairs={{0,1},{1,2},{2,3},{3,4},{4,5},{5,6},{6,7},{7,8},{8,9},{9,10},{10,1... | collective-permute-start | bytes 98312 | tf_op jit(solution)/shard_map/ppermute | solution.py:17
  95.8 20.7 %collective-permute-start.7 = (f32[2,1,32,128]{3,1,0,2:T(1,128)S(1)}, f32[2,1,32,128]{3,1,0,2:T(1,128)S(1)}, u32[]{:S(2)}, u32[]{:S(2)}) collective-permute-start(f32[2,1,32,128]{3,1,0,2:T(1,128)S(1)} %get-tuple-element.180), channel_id=1, source_target_pairs={{1,0},{2,1},{3,2},{4,3},{5,4},{6,5},{7,6},{8,7},{9,8},{10,9},{11,1... | collective-permute-start | bytes 98312 | tf_op jit(solution)/shard_map/ppermute | solution.py:18
  117.5 6.5 %collective-permute-start.8 = (f32[2,1,32,128]{3,1,0,2:T(1,128)S(1)}, f32[2,1,32,128]{3,1,0,2:T(1,128)S(1)}, u32[]{:S(2)}, u32[]{:S(2)}) collective-permute-start(f32[2,1,32,128]{3,1,0,2:T(1,128)S(1)} %get-tuple-element.177), channel_id=1, source_target_pairs={{0,1},{1,2},{2,3},{3,4},{4,5},{5,6},{6,7},{7,8},{8,9},{9,10},{10,1... | collective-permute-start | bytes 98312 | tf_op jit(solution)/shard_map/ppermute | solution.py:17
  119.4 6.1 %collective-permute-start.9 = (f32[2,1,32,128]{3,1,0,2:T(1,128)S(1)}, f32[2,1,32,128]{3,1,0,2:T(1,128)S(1)}, u32[]{:S(2)}, u32[]{:S(2)}) collective-permute-start(f32[2,1,32,128]{3,1,0,2:T(1,128)S(1)} %get-tuple-element.178), channel_id=1, source_target_pairs={{1,0},{2,1},{3,2},{4,3},{5,4},{6,5},{7,6},{8,7},{9,8},{10,9},{11,1... | collective-permute-start | bytes 98312 | tf_op jit(solution)/shard_map/ppermute | solution.py:18
  127.6 11.6 %all-to-all-start.1 = ((bf16[2,2,32,128]{3,1,0,2:T(2,128)(2,1)}), bf16[2,2,32,128]{3,1,0,2:T(2,128)(2,1)S(1)}, u32[]{:S(2)}, u32[]{:S(2)}) async-start(bf16[2,2,32,128]{3,1,0,2:T(2,128)(2,1)} %convert_element_type.75), calls=%async_computation.1 | async-start | bytes 65536 | tf_op jit(solution)/shard_map/all_to_all | solution.py:122
  139.2 11.5 %all-to-all-start = ((bf16[2,2,32,128]{3,1,0,2:T(2,128)(2,1)}), bf16[2,2,32,128]{3,1,0,2:T(2,128)(2,1)S(1)}, u32[]{:S(2)}, u32[]{:S(2)}) async-start(bf16[2,2,32,128]{3,1,0,2:T(2,128)(2,1)} %get-tuple-element.176), calls=%async_computation | async-start | bytes 65536 | tf_op jit(solution)/shard_map/all_to_all | solution.py:122
  144.2 13.2 %collective-permute-start.10 = (bf16[2,32,1,128]{3,1,2,0:T(8,128)(2,1)S(1)}, bf16[2,32,1,128]{3,1,2,0:T(8,128)(2,1)S(1)}, u32[]{:S(2)}, u32[]{:S(2)}) collective-permute-start(bf16[2,32,1,128]{3,1,2,0:T(8,128)(2,1)S(1)} %get-tuple-element.187), channel_id=1, source_target_pairs={{0,1},{1,2},{2,3},{3,4},{4,5},{5,6},{6,7},{7,8},{8,9},{9,10},{10,1... | collective-permute-start | bytes 49160 | tf_op jit(solution)/shard_map/ppermute | solution.py:17
  146.3 11.2 %collective-permute-start.11 = (bf16[2,32,1,128]{3,1,2,0:T(8,128)(2,1)S(1)}, bf16[2,32,1,128]{3,1,2,0:T(8,128)(2,1)S(1)}, u32[]{:S(2)}, u32[]{:S(2)}) collective-permute-start(bf16[2,32,1,128]{3,1,2,0:T(8,128)(2,1)S(1)} %get-tuple-element.188), channel_id=1, source_target_pairs={{1,0},{2,1},{3,2},{4,3},{5,4},{6,5},{7,6},{8,7},{9,8},{10,9},{11,1... | collective-permute-start | bytes 49160 | tf_op jit(solution)/shard_map/ppermute | solution.py:18
  150.8 10.2 %collective-permute-start.4 = (bf16[2,32,1,128]{3,1,2,0:T(8,128)(2,1)S(1)}, bf16[2,32,1,128]{3,1,2,0:T(8,128)(2,1)S(1)}, u32[]{:S(2)}, u32[]{:S(2)}) collective-permute-start(bf16[2,32,1,128]{3,1,2,0:T(8,128)(2,1)S(1)} %get-tuple-element.193), channel_id=1, source_target_pairs={{0,1},{1,2},{2,3},{3,4},{4,5},{5,6},{6,7},{7,8},{8,9},{9,10},{10,1... | collective-permute-start | bytes 49160 | tf_op jit(solution)/shard_map/ppermute | solution.py:17
  152.7 8.3 %collective-permute-start.5 = (bf16[2,32,1,128]{3,1,2,0:T(8,128)(2,1)S(1)}, bf16[2,32,1,128]{3,1,2,0:T(8,128)(2,1)S(1)}, u32[]{:S(2)}, u32[]{:S(2)}) collective-permute-start(bf16[2,32,1,128]{3,1,2,0:T(8,128)(2,1)S(1)} %get-tuple-element.194), channel_id=1, source_target_pairs={{1,0},{2,1},{3,2},{4,3},{5,4},{6,5},{7,6},{8,7},{9,8},{10,9},{11,1... | collective-permute-start | bytes 49160 | tf_op jit(solution)/shard_map/ppermute | solution.py:18
where the time goes:
time: 172 us; the launch traced here: 171 us
  other arithmetic  102 us (59%)
  starting transfers between devices  50.5 us (29%)
  local copies, waits for them, and re-layouts  8.66 us (5%)
  waiting for transfers between devices  7.55 us (4%)
  between operations  2.86 us (2%)
    scatter-add x8, other arithmetic, surface_term(): return jnp.zeros((count + 1,), jnp.float32).at[target].add(values)[:count]  66.3 us
    ppermute x6, starting transfers between devices, extended_2(): after = lax.ppermute(leading, axis, down)  27.3 us
    ppermute x6, starting transfers between devices, extended_2(): before = lax.ppermute(last, axis, up)  11.6 us
    all_to_all x2, starting transfers between devices, shards(): lax.all_to_all(current.astype(jnp.bfloat16), 'tile', split_axis=2, concat...  11.5 us
    select_n x1, other arithmetic, lookup(): result = jnp.where(facies == facies_id, table[facies_id], result)  5.95 us
    unnamed x62, other arithmetic  5.87 us
    dynamic_update_slice x4, other arithmetic, shards(): filtered = lax.map(filter_planes, grouped)  5.57 us
    mul x1, other arithmetic, wave_update(): operator = aniso * (along_x + along_y) + along_z + 0.25 * tilt * mixed  5 us
  transfers between devices with their start and end apart: 14, of which 3 were waited for; matrix products, arithmetic and copies ran while one was open for 55% of the time, Pallas kernels for 0%

commit v1 on v0

v1 whole, which is shorter than its diff:
```python
import functools

import jax
import jax.numpy as jnp
from jax import lax
from jax.experimental import pallas as pl
from jax.experimental.pallas import tpu as pltpu
from jax.sharding import PartitionSpec as P

NLAG = 32
STEPS = 4
HALO = 2
PARTS = 4


def in_order(count, body):
    def run(i, carry):
        body(i)
        return carry

    lax.fori_loop(0, count, run, 0)


def kernel(
    tiles,
    now,
    prev,
    facies,
    vel_tab,
    eps_tab,
    tilt_tab,
    src_cell,
    wavelet,
    cells,
    data,
    out,
    wave_out,
    ext0,
    ext1,
    mid0,
    mid1,
    prev_halo,
    fac_halo,
    coef,
    lhs,
    surf,
    turned,
    send,
    recv,
    planes,
    part_image,
    staged,
    halo_send,
    halo_recv,
    snap_send,
    snap_recv,
):
    rows, depth, cols = facies.shape
    per = depth // tiles
    nrec = data.shape[1]
    ext_rows = rows + 2
    group = 2 * rows
    block = (per + 2) * group
    margin = NLAG // 2
    me = lax.axis_index("tile")
    has_up = me > 0
    has_down = me < tiles - 1

    barrier = pltpu.get_barrier_semaphore()

    def greet(i):
        peer = lax.rem(me + 1 + i, tiles)
        pl.semaphore_signal(barrier, inc=1, device_id={"tile": peer})

    in_order(tiles - 1, greet)

    cell = cells[...]
    column = cell & (cols - 1) if cols & (cols - 1) == 0 else lax.rem(cell, cols)
    onehot = (lax.broadcasted_iota(jnp.int32, (cols, nrec), 0) == column).astype(jnp.float32)
    onehot = onehot.astype(jnp.bfloat16)
    amounts = data[...]
    high = amounts.astype(jnp.bfloat16).astype(jnp.float32)
    rest = amounts - high
    middle = rest.astype(jnp.bfloat16).astype(jnp.float32)
    parts = (high, middle, rest - middle, jnp.zeros_like(high))
    for i in range(ext_rows):
        first = (me * rows + i - 1) * cols
        inside = (cell >= first) & (cell < first + cols)
        for p, part in enumerate(parts):
            at = (i * PARTS + p) * STEPS
            lhs[at : at + STEPS, :] = jnp.where(inside, part, 0.0)
    surf[...] = lax.dot_general(
        lhs[...].astype(jnp.bfloat16), onehot, (((1,), (1,)), ((), ())),
        preferred_element_type=jnp.float32,
    )

    def fill_coef(i, kinds):
        vel = jnp.zeros((depth, cols), jnp.float32)
        eps, tlt = vel, vel
        for n in range(vel_tab.shape[0]):
            here = kinds == n
            vel = jnp.where(here, vel_tab[n], vel)
            eps = jnp.where(here, eps_tab[n], eps)
            tlt = jnp.where(here, tilt_tab[n], tlt)
        coef[0, i] = vel
        coef[1, i] = 1.0 + 2.0 * eps
        coef[2, i] = 0.25 * tlt

    for i in range(rows):
        fill_coef(i + 1, facies[i])
    for f in range(2):
        for i in range(rows):
            ext0[f, i + HALO] = now[f, i]
    zero_plane = jnp.zeros((depth, cols), jnp.float32)
    turned[0:group, :] = jnp.zeros((group, cols), jnp.float32)
    turned[group * (depth + 1) : group * (depth + 2), :] = jnp.zeros((group, cols), jnp.float32)

    def clear_side(side, row):
        for f in range(2):
            for i in range(HALO):
                ext0[f, row + i] = zero_plane
                ext1[f, row + i] = zero_plane
            prev_halo[side, f] = zero_plane
        fac_halo[side] = jnp.full((depth, cols), -1, jnp.int32)

    @pl.when(jnp.logical_not(has_up))
    def _():
        clear_side(0, 0)

    @pl.when(jnp.logical_not(has_down))
    def _():
        clear_side(1, rows + HALO)

    pl.semaphore_wait(barrier, tiles - 1)

    def remote(src, dst, ssem, rsem, peer):
        return pltpu.make_async_remote_copy(
            src_ref=src, dst_ref=dst, send_sem=ssem, recv_sem=rsem, device_id={"tile": peer}
        )

    def halo_copies(side):
        peer = me - 1 if side == 0 else me + 1
        first = 0 if side == 0 else rows - HALO
        edge = 0 if side == 0 else rows - 1
        other = 1 - side
        into = rows + HALO if side == 0 else 0
        sems = lambda n: (halo_send.at[side, n], halo_recv.at[other, n], peer)
        return (
            remote(now.at[:, first : first + HALO], ext0.at[:, into : into + HALO], *sems(0)),
            remote(facies.at[edge], fac_halo.at[other], *sems(1)),
            remote(prev.at[:, edge], prev_halo.at[other], *sems(2)),
        )

    def wave_copy(side):
        peer = me - 1 if side == 0 else me + 1
        first = HALO if side == 0 else rows
        into = rows + HALO if side == 0 else 0
        return remote(
            ext1.at[:, first : first + HALO], ext1.at[:, into : into + HALO],
            halo_send.at[side, 3], halo_recv.at[1 - side, 3], peer,
        )

    def arrivals(side, count):
        into = 0 if side == 0 else rows + HALO
        peer = me
        sems = lambda n: (halo_send.at[side, n], halo_recv.at[side, n], peer)
        if count == 3:
            return (
                remote(now.at[:, 0:HALO], ext0.at[:, into : into + HALO], *sems(0)),
                remote(facies.at[0], fac_halo.at[side], *sems(1)),
                remote(prev.at[:, 0], prev_halo.at[side], *sems(2)),
            )
        return (remote(ext1.at[:, HALO : 2 * HALO], ext1.at[:, into : into + HALO], *sems(3)),)

    def each_side(action):
        for side, there in ((0, has_up), (1, has_down)):
            @pl.when(there)
            def _():
                action(side)

    def start_halo(side):
        for copy in halo_copies(side):
            copy.start()

    def wait_halo(side):
        for copy in arrivals(side, 3):
            copy.wait_recv()

    def wait_wave(side):
        for copy in arrivals(side, 1):
            copy.wait_recv()

    each_side(start_halo)
    each_side(wait_halo)
    fill_coef(0, fac_halo[0])
    fill_coef(rows + 1, fac_halo[1])

    lane = lax.broadcasted_iota(jnp.int32, (depth, cols), 1)
    level = lax.broadcasted_iota(jnp.int32, (depth, cols), 0)
    first_lane, last_lane = lane == 0, lane == cols - 1
    first_level, last_level = level == 0, level == depth - 1
    surface_lane = lax.broadcasted_iota(jnp.int32, (1, cols), 1)

    def advance(step, f, i, current, above, below, old):
        right = lambda v: jnp.where(last_lane, 0.0, pltpu.roll(v, cols - 1, 1))
        left = lambda v: jnp.where(first_lane, 0.0, pltpu.roll(v, 1, 1))
        deeper = jnp.where(last_level, 0.0, pltpu.roll(current, depth - 1, 0))
        higher = jnp.where(first_level, 0.0, pltpu.roll(current, 1, 0))
        twice = 2.0 * current
        along_x = right(current) + left(current) - twice
        along_y = above + below - twice
        along_z = deeper + higher - twice
        slope = deeper - higher
        mixed = right(slope) - left(slope)
        operator = coef[1, i] * (along_x + along_y) + along_z + coef[2, i] * mixed
        new = twice - old + coef[0, i] * operator
        if f == 0:
            target = src_cell[0] - (me * rows + i - 1) * cols
            added = jnp.where(surface_lane == target, wavelet[step], 0.0)
        else:
            at = i * PARTS * STEPS + step
            added = surf[at : at + 1, :]
            for p in range(1, 3):
                added = added + surf[at + p * STEPS : at + p * STEPS + 1, :]
        return new + jnp.where(first_level, added, 0.0)

    def outer_step(step, ext, before, into):
        for f in range(2):
            for i in range(ext_rows):
                into[f, i] = advance(
                    step, f, i, ext[f, i + 1], ext[f, i], ext[f, i + 2], before(f, i)
                )

    def inner_step(step, mid, before, store):
        for f in range(2):
            for i in range(rows):
                new = advance(
                    step, f, i + 1, mid[f, i + 1], mid[f, i], mid[f, i + 2], before[f, i + HALO]
                )
                store(f, i, new)
                turned[pl.ds(group + f * rows + i, depth, stride=group), :] = new

    def prev_row(f, i):
        if i == 0:
            return prev_halo[0, f]
        if i == rows + 1:
            return prev_halo[1, f]
        return prev[f, i - 1]

    def pack_snapshot(s):
        for d in range(tiles):
            at = d * per * group
            send[s, d] = turned[at : at + block, :].astype(jnp.bfloat16)

    def snap_copy(s, peer):
        return remote(
            send.at[s, peer], recv.at[s, me], snap_send.at[s, peer], snap_recv.at[s, me], peer
        )

    def send_snapshot(s):
        in_order(tiles - 1, lambda i: snap_copy(s, lax.rem(me + 1 + i, tiles)).start())
        recv[s, me] = send[s, me]

    def await_snapshot(s):
        def body(i):
            peer = lax.rem(me + 1 + i, tiles)
            remote(
                send.at[s, me], recv.at[s, peer], snap_send.at[s, me], snap_recv.at[s, peer], peer
            ).wait_recv()

        in_order(tiles - 1, body)

    def open_snapshot(s):
        staged[...] = recv[s].reshape(tiles * block, cols).astype(jnp.float32)
        for f in range(2):
            for j in range(per + 2):
                for r in range(rows):
                    at = (j * rows + r) * tiles
                    planes[s, f, at : at + tiles, :] = staged[
                        pl.ds(j * group + f * rows + r, tiles, stride=block), :
                    ]

    outer_step(0, ext0, prev_row, mid0)

    def keep_ext1(f, i, new):
        ext1[f, i + HALO] = new

    inner_step(1, mid0, ext0, keep_ext1)
    each_side(lambda side: wave_copy(side).start())
    pack_snapshot(0)
    send_snapshot(0)
    each_side(wait_wave)
    outer_step(2, ext1, lambda f, i: mid0[f, i], mid1)

    def keep_out(f, i, new):
        wave_out[f, i] = new

    inner_step(3, mid1, ext1, keep_out)
    pack_snapshot(1)
    send_snapshot(1)

    await_snapshot(0)
    open_snapshot(0)

    def pulled(s, k):
        shift = lax.rem(2 * margin - 2 * k + 2 * cols, cols)
        return planes[s, 0] * pltpu.roll(planes[s, 1], shift, 1)

    def first_products(k):
        part_image[k] = pulled(0, k)

    in_order(NLAG, first_products)
    await_snapshot(1)
    open_snapshot(1)

    image_rows = (per + 2) * rows * tiles
    plane_rows = rows * tiles
    image_lane = lax.broadcasted_iota(jnp.int32, (1, cols), 1)
    tile_index = lax.broadcasted_iota(jnp.int32, (tiles, cols), 0)

    def finish(k):
        h = k - margin
        far = image_lane + 2 * h
        valid = (far >= 0) & (far < cols)
        image = jnp.where(valid, part_image[k] + pulled(1, k), 0.0)
        image = image.astype(jnp.bfloat16).astype(jnp.float32)
        own = image[plane_rows : plane_rows * (per + 1)]
        at_first = image_lane == lax.rem(cols - h, cols)
        at_last = image_lane == lax.rem(2 * cols - 1 - h, cols)
        total = jnp.where(at_first, 0.0, pltpu.roll(own, 1, 1))
        total = total + jnp.where(at_last, 0.0, pltpu.roll(own, cols - 1, 1))
        total = total + image[: plane_rows * per] + image[2 * plane_rows :]
        pieces = []
        for z in range(per):
            for r in range(rows):
                here = lambda q: own[z * plane_rows + q * tiles : z * plane_rows + (q + 1) * tiles]
                if r > 0:
                    low = here(r - 1)
                else:
                    low = jnp.where(tile_index == 0, 0.0, pltpu.roll(here(rows - 1), 1, 0))
                if r < rows - 1:
                    high = here(r + 1)
                else:
                    high = jnp.where(
                        tile_index == tiles - 1, 0.0, pltpu.roll(here(0), tiles - 1, 0)
                    )
                pieces.append(low + high)
        total = total + jnp.concatenate(pieces, axis=0)
        result = 0.125 * (6.0 * own - total)
        result = pltpu.roll(result, lax.rem(h + cols, cols), 1)
        for z in range(per):
            for r in range(rows):
                at = z * plane_rows + r * tiles
                staged[pl.ds(r * per + z, tiles, stride=rows * per), :] = result[at : at + tiles]
        out[k] = staged[0 : plane_rows * per, :].astype(jnp.bfloat16)

    in_order(NLAG, finish)

    def sent(side):
        for copy in halo_copies(side):
            copy.wait_send()
        wave_copy(side).wait_send()

    each_side(sent)
    for s in range(2):
        in_order(tiles - 1, lambda i: snap_copy(s, lax.rem(me + 1 + i, tiles)).wait_send())


def shards(tiles, now, prev, facies, vel, eps, tilt, src_cell, wavelet, cells, data):
    rows, depth, cols = facies.shape
    per = depth // tiles
    nrec = cells.shape[0]
    block = (per + 2) * 2 * rows
    image_rows = (per + 2) * rows * tiles
    f32 = jnp.float32
    vmem = pl.BlockSpec(memory_space=pltpu.VMEM)
    smem = pl.BlockSpec(memory_space=pltpu.SMEM)
    lhs_rows = (rows + 2) * PARTS * STEPS
    filtered, wave = pl.pallas_call(
        functools.partial(kernel, tiles),
        out_shape=(
            jax.ShapeDtypeStruct((NLAG, rows * tiles * per, cols), jnp.bfloat16),
            jax.ShapeDtypeStruct(now.shape, f32),
        ),
        in_specs=[vmem] * 3 + [smem] * 5 + [vmem] * 2,
        out_specs=(vmem, vmem),
        scratch_shapes=[
            pltpu.VMEM((2, rows + 2 * HALO, depth, cols), f32),
            pltpu.VMEM((2, rows + 2 * HALO, depth, cols), f32),
            pltpu.VMEM((2, rows + 2, depth, cols), f32),
            pltpu.VMEM((2, rows + 2, depth, cols), f32),
            pltpu.VMEM((2, 2, depth, cols), f32),
            pltpu.VMEM((2, depth, cols), jnp.int32),
            pltpu.VMEM((3, rows + 2, depth, cols), f32),
            pltpu.VMEM((lhs_rows, nrec), f32),
            pltpu.VMEM((lhs_rows, cols), f32),
            pltpu.VMEM((2 * rows * (depth + 2), cols), f32),
            pltpu.VMEM((2, tiles, block, cols), jnp.bfloat16),
            pltpu.VMEM((2, tiles, block, cols), jnp.bfloat16),
            pltpu.VMEM((2, 2, image_rows, cols), f32),
            pltpu.VMEM((NLAG, image_rows, cols), f32),
            pltpu.VMEM((tiles * block, cols), f32),
            pltpu.SemaphoreType.DMA((2, 4)),
            pltpu.SemaphoreType.DMA((2, 4)),
            pltpu.SemaphoreType.DMA((2, tiles)),
            pltpu.SemaphoreType.DMA((2, tiles)),
        ],
        compiler_params=pltpu.CompilerParams(collective_id=0, has_side_effects=True),
    )(now, prev, facies, vel, eps, tilt, src_cell, wavelet, cells.reshape(1, nrec), data)
    return filtered.reshape(NLAG, rows * tiles, per, cols), wave


def solution(mesh):
    return jax.shard_map(
        functools.partial(shards, mesh.shape["tile"]),
        mesh=mesh,
        in_specs=(
            P("shot", "tile", None, None),
            P("shot", "tile", None, None),
            P("tile", None, None),
            P(),
            P(),
            P(),
            P("shot"),
            P("shot"),
            P("shot"),
            P(None, "shot"),
        ),
        out_specs=(P("shot", None, "tile", None), P("shot", "tile", None, None)),
        check_vma=False,
    )
```

time: 172 us -> 32.9 us (0.19)
  the two profiles are of different devices: /device:TPU:8 before, /device:TPU:0 now
where the time goes in v1:
time: 32.9 us; the launch traced here: 32.7 us
  Pallas kernels  28.5 us (87%)
  local copies, waits for them, and re-layouts  2.94 us (9%)
  between operations  1.3 us (4%)
    pallas_call x1, Pallas kernels, shards(): pl.pallas_call(functools.partial(kernel, tiles), out_shape=(jax.ShapeDtyp...  28.5 us
    unnamed x4, local copies, waits for them, and re-layouts  2.94 us

profile of v1, /device:TPU:0, one launch (start us, length us, event | category | flops | bytes accessed | tf_op | source)
XLA Modules:
  0.0 32.7 jit_solution(15652239645218410025)
XLA Ops:
  1.3 28.5 %shard_map.113 = (bf16[32,64,128]{2,1,0:T(8,128)(2,1)}, f32[2,2,32,128]{3,2,1,0:T(8,128)}) custom-call(f32[2,2,32,128]{3,2,1,0:T(8,128)} %now.1, f32[2,2,32,128]{3,2,1,0:T(8,128)} %prev.1, s32[2,32,128]{2,1,0:T(8,128)} %facies.1, f32[8]{0:T(128)} %vel_tab.1, f32[8]{0:T(128)} %eps_tab.1, f32[8]{0:T(128)} %tilt_tab.1, s32[1]{0:T(128)S(6)} %copy.14.src_cell, ...), custom_call_target="tpu_custom_call" | custom-call | tf_op jit(solution)/shard_map/pallas_call | solution.py:379
  29.8 0.0 copy-start
  29.8 2.3 %copy.15 = bf16[32,32,2,128]{3,2,1,0:T(2,128)(2,1)} copy(bf16[32,32,2,128]{3,2,1,0:T(2,128)(2,1)} %bitcast.2) | data formatting | bytes 1048576
  32.1 0.0 copy-done
  32.1 0.6 %copy.16 = f32[2,2,32,128]{3,2,1,0:T(8,128)} copy(f32[2,2,32,128]{3,2,1,0:T(8,128)S(1)} %copy-done) | data formatting | bytes 131072
Async XLA Ops:
  29.8 2.3 %copy-start = (f32[2,2,32,128]{3,2,1,0:T(8,128)S(1)}, f32[2,2,32,128]{3,2,1,0:T(8,128)}, u32[]{:S(2)}) copy-start(f32[2,2,32,128]{3,2,1,0:T(8,128)} %get-tuple-element.9) | copy-start | bytes 196612

commit v2 on v1

--- a/solution.py
+++ b/solution.py
@@ -10,6 +10,8 @@
 NLAG = 32
 STEPS = 4
 HALO = 2
+UNROLL = 4
+REACH = 4
 PARTS = 4
 
 
@@ -24,6 +26,17 @@
 def kernel(
     tiles,
     now,
+    prev_in,
+    facies_in,
+    vel_in,
+    eps_in,
+    tilt_in,
+    src_in,
+    wavelet_in,
+    cells_in,
+    data_in,
+    out_hbm,
+    wave_hbm,
     prev,
     facies,
     vel_tab,
@@ -50,10 +63,14 @@
     planes,
     part_image,
     staged,
+    woven,
     halo_send,
     halo_recv,
     snap_send,
     snap_recv,
+    load_sem,
+    store_sem,
+    near_sem,
 ):
     rows, depth, cols = facies.shape
     per = depth // tiles
@@ -68,11 +85,129 @@
 
     barrier = pltpu.get_barrier_semaphore()
 
-    def greet(i):
-        peer = lax.rem(me + 1 + i, tiles)
-        pl.semaphore_signal(barrier, inc=1, device_id={"tile": peer})
-
-    in_order(tiles - 1, greet)
+    def signal_at(semaphore, step):
+        for way in (-step, step):
+            peer = me + way
+            there = (peer >= 0) & (peer < tiles)
+
+            @pl.when(there)
+            def _():
+                pl.semaphore_signal(semaphore, inc=1, device_id={"tile": peer})
+
+    def wait_at(semaphore, step):
+        lower = (me >= step).astype(jnp.int32)
+        pl.semaphore_wait(semaphore, lower + (me + step < tiles).astype(jnp.int32))
+
+    near = range(1, min(REACH, tiles - 1) + 1)
+    for step in near:
+        signal_at(barrier, step)
+
+    reaches = []
+    while (REACH << len(reaches)) < tiles - 1:
+        reaches.append(REACH << len(reaches))
+
+    loads = [
+        pltpu.make_async_copy(src, dst, load_sem.at[n])
+        for n, (src, dst) in enumerate(
+            (
+                (cells_in, cells),
+                (data_in, data),
+                (facies_in, facies),
+                (vel_in, vel_tab),
+                (eps_in, eps_tab),
+                (tilt_in, tilt_tab),
+                (src_in, src_cell),
+                (wavelet_in, wavelet),
+                (now, ext0.at[:, HALO : HALO + rows]),
+                (prev_in, prev),
+            )
+        )
+    ]
+    for load in loads:
+        load.start()
+    zero_plane = jnp.zeros((depth, cols), jnp.float32)
+    def clear_side(side, row):
+        for f in range(2):
+            for i in range(HALO):
+                ext0[f, row + i] = zero_plane
+                ext1[f, row + i] = zero_plane
+            prev_halo[side, f] = zero_plane
+        fac_halo[side] = jnp.full((depth, cols), -1, jnp.int32)
+
+    @pl.when(jnp.logical_not(has_up))
+    def _():
+        clear_side(0, 0)
+
+    @pl.when(jnp.logical_not(has_down))
+    def _():
+        clear_side(1, rows + HALO)
+
+    reach = min(REACH, tiles - 1)
+    pl.semaphore_wait(barrier, jnp.minimum(me, reach) + jnp.minimum(tiles - 1 - me, reach))
+
+    def remote(src, dst, ssem, rsem, peer):
+        return pltpu.make_async_remote_copy(
+            src_ref=src, dst_ref=dst, send_sem=ssem, recv_sem=rsem, device_id={"tile": peer}
+        )
+
+    def halo_copies(side):
+        peer = me - 1 if side == 0 else me + 1
+        first = 0 if side == 0 else rows - HALO
+        edge = 0 if side == 0 else rows - 1
+        other = 1 - side
+        into = rows + HALO if side == 0 else 0
+        sems = lambda n: (halo_send.at[side, n], halo_recv.at[other, n], peer)
+        return (
+            remote(now.at[:, first : first + HALO], ext0.at[:, into : into + HALO], *sems(0)),
+            remote(facies_in.at[edge], fac_halo.at[other], *sems(1)),
+            remote(prev_in.at[:, edge], prev_halo.at[other], *sems(2)),
+        )
+
+    def wave_copy(side):
+        peer = me - 1 if side == 0 else me + 1
+        first = HALO if side == 0 else rows
+        into = rows + HALO if side == 0 else 0
+        return remote(
+            ext1.at[:, first : first + HALO], ext1.at[:, into : into + HALO],
+            halo_send.at[side, 3], halo_recv.at[1 - side, 3], peer,
+        )
+
+    def arrivals(side, count):
+        into = 0 if side == 0 else rows + HALO
+        peer = me
+        sems = lambda n: (halo_send.at[side, n], halo_recv.at[side, n], peer)
+        if count == 3:
+            return (
+                remote(now.at[:, 0:HALO], ext0.at[:, into : into + HALO], *sems(0)),
+                remote(facies_in.at[0], fac_halo.at[side], *sems(1)),
+                remote(prev_in.at[:, 0], prev_halo.at[side], *sems(2)),
+            )
+        return (remote(ext1.at[:, HALO : 2 * HALO], ext1.at[:, into : into + HALO], *sems(3)),)
+
+    def each_side(action):
+        for side, there in ((0, has_up), (1, has_down)):
+            @pl.when(there)
+            def _():
+                action(side)
+
+    def start_halo(side):
+        for copy in halo_copies(side):
+            copy.start()
+
+    def wait_halo(side):
+        for copy in arrivals(side, 3):
+            copy.wait_recv()
+
+    def wait_wave(side):
+        for copy in arrivals(side, 1):
+            copy.wait_recv()
+
+    each_side(start_halo)
+    if reaches:
+        signal_at(near_sem.at[0], reaches[0])
+
+    for load in loads[:2]:
+        load.wait()
 
     cell = cells[...]
     column = cell & (cols - 1) if cols & (cols - 1) == 0 else lax.rem(cell, cols)
@@ -106,92 +241,18 @@
         coef[1, i] = 1.0 + 2.0 * eps
         coef[2, i] = 0.25 * tlt
 
+    for load in loads[2:]:
+        load.wait()
     for i in range(rows):
         fill_coef(i + 1, facies[i])
-    for f in range(2):
-        for i in range(rows):
-            ext0[f, i + HALO] = now[f, i]
-    zero_plane = jnp.zeros((depth, cols), jnp.float32)
     turned[0:group, :] = jnp.zeros((group, cols), jnp.float32)
     turned[group * (depth + 1) : group * (depth + 2), :] = jnp.zeros((group, cols), jnp.float32)
 
-    def clear_side(side, row):
-        for f in range(2):
-            for i in range(HALO):
-                ext0[f, row + i] = zero_plane
-                ext1[f, row + i] = zero_plane
-            prev_halo[side, f] = zero_plane
-        fac_halo[side] = jnp.full((depth, cols), -1, jnp.int32)
-
-    @pl.when(jnp.logical_not(has_up))
-    def _():
-        clear_side(0, 0)
-
-    @pl.when(jnp.logical_not(has_down))
-    def _():
-        clear_side(1, rows + HALO)
-
-    pl.semaphore_wait(barrier, tiles - 1)
-
-    def remote(src, dst, ssem, rsem, peer):
-        return pltpu.make_async_remote_copy(
-            src_ref=src, dst_ref=dst, send_sem=ssem, recv_sem=rsem, device_id={"tile": peer}
-        )
-
-    def halo_copies(side):
-        peer = me - 1 if side == 0 else me + 1
-        first = 0 if side == 0 else rows - HALO
-        edge = 0 if side == 0 else rows - 1
-        other = 1 - side
-        into = rows + HALO if side == 0 else 0
-        sems = lambda n: (halo_send.at[side, n], halo_recv.at[other, n], peer)
-        return (
-            remote(now.at[:, first : first + HALO], ext0.at[:, into : into + HALO], *sems(0)),
-            remote(facies.at[edge], fac_halo.at[other], *sems(1)),
-            remote(prev.at[:, edge], prev_halo.at[other], *sems(2)),
-        )
-
-    def wave_copy(side):
-        peer = me - 1 if side == 0 else me + 1
-        first = HALO if side == 0 else rows
-        into = rows + HALO if side == 0 else 0
-        return remote(
-            ext1.at[:, first : first + HALO], ext1.at[:, into : into + HALO],
-            halo_send.at[side, 3], halo_recv.at[1 - side, 3], peer,
-        )
-
-    def arrivals(side, count):
-        into = 0 if side == 0 else rows + HALO
-        peer = me
-        sems = lambda n: (halo_send.at[side, n], halo_recv.at[side, n], peer)
-        if count == 3:
-            return (
-                remote(now.at[:, 0:HALO], ext0.at[:, into : into + HALO], *sems(0)),
-                remote(facies.at[0], fac_halo.at[side], *sems(1)),
-                remote(prev.at[:, 0], prev_halo.at[side], *sems(2)),
-            )
-        return (remote(ext1.at[:, HALO : 2 * HALO], ext1.at[:, into : into + HALO], *sems(3)),)
-
-    def each_side(action):
-        for side, there in ((0, has_up), (1, has_down)):
-            @pl.when(there)
-            def _():
-                action(side)
-
-    def start_halo(side):
-        for copy in halo_copies(side):
-            copy.start()
-
-    def wait_halo(side):
-        for copy in arrivals(side, 3):
-            copy.wait_recv()
-
-    def wait_wave(side):
-        for copy in arrivals(side, 1):
-            copy.wait_recv()
-
-    each_side(start_halo)
     each_side(wait_halo)
+    if reaches:
+        wait_at(near_sem.at[0], reaches[0])
+    if len(reaches) > 1:
+        signal_at(near_sem.at[1], reaches[1])
     fill_coef(0, fac_halo[0])
     fill_coef(rows + 1, fac_halo[1])
 
@@ -288,8 +349,12 @@
     inner_step(1, mid0, ext0, keep_ext1)
     each_side(lambda side: wave_copy(side).start())
     pack_snapshot(0)
+    each_side(wait_wave)
+    for n in range(1, len(reaches)):
+        wait_at(near_sem.at[n], reaches[n])
+        if n + 1 < len(reaches):
+            signal_at(near_sem.at[n + 1], reaches[n + 1])
     send_snapshot(0)
-    each_side(wait_wave)
     outer_step(2, ext1, lambda f, i: mid0[f, i], mid1)
 
     def keep_out(f, i, new):
@@ -298,6 +363,8 @@
     inner_step(3, mid1, ext1, keep_out)
     pack_snapshot(1)
     send_snapshot(1)
+    wave_store = pltpu.make_async_copy(wave_out, wave_hbm, store_sem.at[NLAG // UNROLL])
+    wave_store.start()
 
     await_snapshot(0)
     open_snapshot(0)
@@ -318,7 +385,7 @@
     image_lane = lax.broadcasted_iota(jnp.int32, (1, cols), 1)
     tile_index = lax.broadcasted_iota(jnp.int32, (tiles, cols), 0)
 
-    def finish(k):
+    def finish(u, k):
         h = k - margin
         far = image_lane + 2 * h
         valid = (far >= 0) & (far < cols)
@@ -351,10 +418,21 @@
         for z in range(per):
             for r in range(rows):
                 at = z * plane_rows + r * tiles
-                staged[pl.ds(r * per + z, tiles, stride=rows * per), :] = result[at : at + tiles]
-        out[k] = staged[0 : plane_rows * per, :].astype(jnp.bfloat16)
-
-    in_order(NLAG, finish)
+                woven[u, pl.ds(r * per + z, tiles, stride=rows * per), :] = result[at : at + tiles]
+        out[k] = woven[u].astype(jnp.bfloat16)
+
+    def stored(b):
+        span = pl.ds(b * UNROLL, UNROLL)
+        return pltpu.make_async_copy(out.at[span], out_hbm.at[span], store_sem.at[b])
+
+    def finish_some(b):
+        for u in range(UNROLL):
+            finish(u, b * UNROLL + u)
+        stored(b).start()
+
+    in_order(NLAG // UNROLL, finish_some)
+    in_order(NLAG // UNROLL, lambda b: stored(b).wait())
+    wave_store.wait()
 
     def sent(side):
         for copy in halo_copies(side):
@@ -373,8 +451,7 @@
     block = (per + 2) * 2 * rows
     image_rows = (per + 2) * rows * tiles
     f32 = jnp.float32
-    vmem = pl.BlockSpec(memory_space=pltpu.VMEM)
-    smem = pl.BlockSpec(memory_space=pltpu.SMEM)
+    hbm = pl.BlockSpec(memory_space=pltpu.HBM)
     lhs_rows = (rows + 2) * PARTS * STEPS
     filtered, wave = pl.pallas_call(
         functools.partial(kernel, tiles),
@@ -382,9 +459,20 @@
             jax.ShapeDtypeStruct((NLAG, rows * tiles * per, cols), jnp.bfloat16),
             jax.ShapeDtypeStruct(now.shape, f32),
         ),
-        in_specs=[vmem] * 3 + [smem] * 5 + [vmem] * 2,
-        out_specs=(vmem, vmem),
+        in_specs=[hbm] * 10,
+        out_specs=(hbm, hbm),
         scratch_shapes=[
+            pltpu.VMEM(prev.shape, f32),
+            pltpu.VMEM(facies.shape, jnp.int32),
+            pltpu.SMEM(vel.shape, f32),
+            pltpu.SMEM(eps.shape, f32),
+            pltpu.SMEM(tilt.shape, f32),
+            pltpu.SMEM(src_cell.shape, jnp.int32),
+            pltpu.SMEM(wavelet.shape, f32),
+            pltpu.VMEM((1, nrec), jnp.int32),
+            pltpu.VMEM(data.shape, f32),
+            pltpu.VMEM((NLAG, rows * tiles * per, cols), jnp.bfloat16),
+            pltpu.VMEM(now.shape, f32),
             pltpu.VMEM((2, rows + 2 * HALO, depth, cols), f32),
             pltpu.VMEM((2, rows + 2 * HALO, depth, cols), f32),
             pltpu.VMEM((2, rows + 2, depth, cols), f32),
@@ -400,10 +488,14 @@
             pltpu.VMEM((2, 2, image_rows, cols), f32),
             pltpu.VMEM((NLAG, image_rows, cols), f32),
             pltpu.VMEM((tiles * block, cols), f32),
+            pltpu.VMEM((UNROLL, rows * tiles * per, cols), f32),
             pltpu.SemaphoreType.DMA((2, 4)),
             pltpu.SemaphoreType.DMA((2, 4)),
             pltpu.SemaphoreType.DMA((2, tiles)),
             pltpu.SemaphoreType.DMA((2, tiles)),
+            pltpu.SemaphoreType.DMA((10,)),
+            pltpu.SemaphoreType.DMA((NLAG // UNROLL + 1,)),
+            pltpu.SemaphoreType.REGULAR((max(1, tiles.bit_length()),)),
         ],
         compiler_params=pltpu.CompilerParams(collective_id=0, has_side_effects=True),
     )(now, prev, facies, vel, eps, tilt, src_cell, wavelet, cells.reshape(1, nrec), data)

time: 32.9 us -> 28 us (0.85)
  Pallas kernels: 28.5 us -> 23.6 us
    pallas_call x1, Pallas kernels: 28.5 us -> 23.6 us  [shards(): pl.pallas_call(functools.partial(kernel, tiles), out_shape=(jax.ShapeDtyp...]
where the time goes in v2:
time: 28 us; the launch traced here: 27.9 us
  Pallas kernels  23.6 us (84%)
  local copies, waits for them, and re-layouts  2.94 us (10%)
  between operations  1.3 us (5%)
    pallas_call x1, Pallas kernels, shards(): pl.pallas_call(functools.partial(kernel, tiles), out_shape=(jax.ShapeDtyp...  23.6 us
    unnamed x4, local copies, waits for them, and re-layouts  2.94 us

profile of v2, /device:TPU:0, one launch (start us, length us, event | category | flops | bytes accessed | tf_op | source)
XLA Modules:
  0.0 27.9 jit_solution(15163198193828491526)
XLA Ops:
  1.3 23.6 %shard_map.113 = (bf16[32,64,128]{2,1,0:T(8,128)(2,1)}, f32[2,2,32,128]{3,2,1,0:T(8,128)}) custom-call(f32[2,2,32,128]{3,2,1,0:T(8,128)} %now.1, f32[2,2,32,128]{3,2,1,0:T(8,128)} %prev_in.1, s32[2,32,128]{2,1,0:T(8,128)} %facies_in.1, f32[8]{0:T(128)} %vel_in.1, f32[8]{0:T(128)} %eps_in.1, f32[8]{0:T(128)} %tilt_in.1, s32[1]{0:T(128)S(6)} %copy.14.src_in, ...), custom_call_target="tpu_custom_call" | custom-call | tf_op jit(solution)/shard_map/pallas_call | solution.py:456
  24.9 0.0 copy-start
  24.9 2.3 %copy.15 = bf16[32,32,2,128]{3,2,1,0:T(2,128)(2,1)} copy(bf16[32,32,2,128]{3,2,1,0:T(2,128)(2,1)} %bitcast.2) | data formatting | bytes 1048576
  27.2 0.0 copy-done
  27.2 0.6 %copy.16 = f32[2,2,32,128]{3,2,1,0:T(8,128)} copy(f32[2,2,32,128]{3,2,1,0:T(8,128)S(1)} %copy-done) | data formatting | bytes 131072
Async XLA Ops:
  24.9 2.3 %copy-start = (f32[2,2,32,128]{3,2,1,0:T(8,128)S(1)}, f32[2,2,32,128]{3,2,1,0:T(8,128)}, u32[]{:S(2)}) copy-start(f32[2,2,32,128]{3,2,1,0:T(8,128)} %get-tuple-element.9) | copy-start | bytes 196612

commit v3 on v2

--- a/solution.py
+++ b/solution.py
@@ -202,9 +202,9 @@
         for copy in arrivals(side, 1):
             copy.wait_recv()
 
-    each_side(start_halo)
     if reaches:
         signal_at(near_sem.at[0], reaches[0])
+    each_side(start_halo)
 
     for load in loads[:2]:
         load.wait()
@@ -349,12 +349,12 @@
     inner_step(1, mid0, ext0, keep_ext1)
     each_side(lambda side: wave_copy(side).start())
     pack_snapshot(0)
-    each_side(wait_wave)
     for n in range(1, len(reaches)):
         wait_at(near_sem.at[n], reaches[n])
         if n + 1 < len(reaches):
             signal_at(near_sem.at[n + 1], reaches[n + 1])
     send_snapshot(0)
+    each_side(wait_wave)
     outer_step(2, ext1, lambda f, i: mid0[f, i], mid1)
 
     def keep_out(f, i, new):
@@ -413,7 +413,7 @@
                     )
                 pieces.append(low + high)
         total = total + jnp.concatenate(pieces, axis=0)
-        result = 0.125 * (6.0 * own - total)
+        result = 6.0 * own - total
         result = pltpu.roll(result, lax.rem(h + cols, cols), 1)
         for z in range(per):
             for r in range(rows):
@@ -499,6 +499,7 @@
         ],
         compiler_params=pltpu.CompilerParams(collective_id=0, has_side_effects=True),
     )(now, prev, facies, vel, eps, tilt, src_cell, wavelet, cells.reshape(1, nrec), data)
+    filtered = filtered * jnp.bfloat16(0.125)
     return filtered.reshape(NLAG, rows * tiles, per, cols), wave
 
 

time: 28 us -> 25.2 us (0.900)
  Pallas kernels: 23.6 us -> 21.2 us
  local copies, waits for them, and re-layouts: 2.94 us -> 0.63 us
  other arithmetic: 0 us -> 1.91 us
    pallas_call x1, Pallas kernels: 23.6 us -> 21.2 us  [shards(): pl.pallas_call(functools.partial(kernel, tiles), out_shape=(jax.ShapeDtyp...]
    unnamed x4 -> x3, local copies, waits for them, and re-layouts: 2.94 us -> 0.63 us
    mul x0 -> x1, other arithmetic: none -> 1.91 us  [shards(): filtered = filtered * jnp.bfloat16(0.125)]
where the time goes in v3:
time: 25.2 us; the launch traced here: 25 us
  Pallas kernels  21.2 us (84%)
  other arithmetic  1.91 us (8%)
  between operations  1.3 us (5%)
  local copies, waits for them, and re-layouts  0.63 us (2%)
    pallas_call x1, Pallas kernels, shards(): pl.pallas_call(functools.partial(kernel, tiles), out_shape=(jax.ShapeDtyp...  21.2 us
    mul x1, other arithmetic, shards(): filtered = filtered * jnp.bfloat16(0.125)  1.91 us
    unnamed x3, local copies, waits for them, and re-layouts  0.63 us

profile of v3, /device:TPU:0, one launch (start us, length us, event | category | flops | bytes accessed | tf_op | source)
XLA Modules:
  0.0 25.0 jit_solution(5685227955048593344)
XLA Ops:
  1.3 21.2 %shard_map.113 = (bf16[32,64,128]{2,1,0:T(8,128)(2,1)}, f32[2,2,32,128]{3,2,1,0:T(8,128)}) custom-call(f32[2,2,32,128]{3,2,1,0:T(8,128)} %now.1, f32[2,2,32,128]{3,2,1,0:T(8,128)} %prev_in.1, s32[2,32,128]{2,1,0:T(8,128)} %facies_in.1, f32[8]{0:T(128)} %vel_in.1, f32[8]{0:T(128)} %eps_in.1, f32[8]{0:T(128)} %tilt_in.1, s32[1]{0:T(128)S(6)} %copy.13.src_in, ...), custom_call_target="tpu_custom_call" | custom-call | tf_op jit(solution)/shard_map/pallas_call | solution.py:456
  22.4 0.0 copy-start
  22.5 1.9 %broadcast_multiply_fusion = bf16[32,64,128]{2,1,0:T(8,128)(2,1)} fusion(bf16[32,64,128]{2,1,0:T(8,128)(2,1)} %get-tuple-element.4), kind=kLoop, calls=%fused_computation | loop fusion | flops 262144 | bytes 1048576 | tf_op jit(solution)/shard_map/mul | solution.py:502
  24.4 0.0 copy-done
  24.4 0.6 %copy.14 = f32[2,2,32,128]{3,2,1,0:T(8,128)} copy(f32[2,2,32,128]{3,2,1,0:T(8,128)S(1)} %copy-done) | data formatting | bytes 131072
Async XLA Ops:
  22.4 1.9 %copy-start = (f32[2,2,32,128]{3,2,1,0:T(8,128)S(1)}, f32[2,2,32,128]{3,2,1,0:T(8,128)}, u32[]{:S(2)}) copy-start(f32[2,2,32,128]{3,2,1,0:T(8,128)} %get-tuple-element.9) | copy-start | bytes 196612

commit v4 on v3

--- a/solution.py
+++ b/solution.py
@@ -35,8 +35,8 @@
     wavelet_in,
     cells_in,
     data_in,
-    out_hbm,
-    wave_hbm,
+    out,
+    wave_out,
     prev,
     facies,
     vel_tab,
@@ -46,8 +46,6 @@
     wavelet,
     cells,
     data,
-    out,
-    wave_out,
     ext0,
     ext1,
     mid0,
@@ -69,7 +67,6 @@
     snap_send,
     snap_recv,
     load_sem,
-    store_sem,
     near_sem,
 ):
     rows, depth, cols = facies.shape
@@ -363,8 +360,6 @@
     inner_step(3, mid1, ext1, keep_out)
     pack_snapshot(1)
     send_snapshot(1)
-    wave_store = pltpu.make_async_copy(wave_out, wave_hbm, store_sem.at[NLAG // UNROLL])
-    wave_store.start()
 
     await_snapshot(0)
     open_snapshot(0)
@@ -413,7 +408,7 @@
                     )
                 pieces.append(low + high)
         total = total + jnp.concatenate(pieces, axis=0)
-        result = 6.0 * own - total
+        result = 0.125 * (6.0 * own - total)
         result = pltpu.roll(result, lax.rem(h + cols, cols), 1)
         for z in range(per):
             for r in range(rows):
@@ -421,18 +416,11 @@
                 woven[u, pl.ds(r * per + z, tiles, stride=rows * per), :] = result[at : at + tiles]
         out[k] = woven[u].astype(jnp.bfloat16)
 
-    def stored(b):
-        span = pl.ds(b * UNROLL, UNROLL)
-        return pltpu.make_async_copy(out.at[span], out_hbm.at[span], store_sem.at[b])
-
     def finish_some(b):
         for u in range(UNROLL):
             finish(u, b * UNROLL + u)
-        stored(b).start()
 
     in_order(NLAG // UNROLL, finish_some)
-    in_order(NLAG // UNROLL, lambda b: stored(b).wait())
-    wave_store.wait()
 
     def sent(side):
         for copy in halo_copies(side):
@@ -451,16 +439,17 @@
     block = (per + 2) * 2 * rows
     image_rows = (per + 2) * rows * tiles
     f32 = jnp.float32
+    vmem = pl.BlockSpec(memory_space=pltpu.VMEM)
     hbm = pl.BlockSpec(memory_space=pltpu.HBM)
     lhs_rows = (rows + 2) * PARTS * STEPS
     filtered, wave = pl.pallas_call(
         functools.partial(kernel, tiles),
         out_shape=(
-            jax.ShapeDtypeStruct((NLAG, rows * tiles * per, cols), jnp.bfloat16),
-            jax.ShapeDtypeStruct(now.shape, f32),
+            pltpu.VMEM((NLAG, rows * tiles * per, cols), jnp.bfloat16),
+            pltpu.VMEM(now.shape, f32),
         ),
         in_specs=[hbm] * 10,
-        out_specs=(hbm, hbm),
+        out_specs=(vmem, vmem),
         scratch_shapes=[
             pltpu.VMEM(prev.shape, f32),
             pltpu.VMEM(facies.shape, jnp.int32),
@@ -471,8 +460,6 @@
             pltpu.SMEM(wavelet.shape, f32),
             pltpu.VMEM((1, nrec), jnp.int32),
             pltpu.VMEM(data.shape, f32),
-            pltpu.VMEM((NLAG, rows * tiles * per, cols), jnp.bfloat16),
-            pltpu.VMEM(now.shape, f32),
             pltpu.VMEM((2, rows + 2 * HALO, depth, cols), f32),
             pltpu.VMEM((2, rows + 2 * HALO, depth, cols), f32),
             pltpu.VMEM((2, rows + 2, depth, cols), f32),
@@ -494,12 +481,10 @@
             pltpu.SemaphoreType.DMA((2, tiles)),
             pltpu.SemaphoreType.DMA((2, tiles)),
             pltpu.SemaphoreType.DMA((10,)),
-            pltpu.SemaphoreType.DMA((NLAG // UNROLL + 1,)),
             pltpu.SemaphoreType.REGULAR((max(1, tiles.bit_length()),)),
         ],
         compiler_params=pltpu.CompilerParams(collective_id=0, has_side_effects=True),
     )(now, prev, facies, vel, eps, tilt, src_cell, wavelet, cells.reshape(1, nrec), data)
-    filtered = filtered * jnp.bfloat16(0.125)
     return filtered.reshape(NLAG, rows * tiles, per, cols), wave
 
 

time: 25.2 us -> 23.4 us (0.929)
  other arithmetic: 1.91 us -> 0 us
  local copies, waits for them, and re-layouts: 0.63 us -> 1.42 us
  Pallas kernels: 21.2 us -> 20.5 us
    mul x1 -> x0, other arithmetic: 1.91 us -> none  [shards(): filtered = filtered * jnp.bfloat16(0.125)]
    unnamed x3 -> x2, local copies, waits for them, and re-layouts: 0.63 us -> 1.42 us
    pallas_call x1, Pallas kernels: 21.2 us -> 20.5 us  [shards(): pl.pallas_call(functools.partial(kernel, tiles), out_shape=(pltpu.VMEM((N...]
where the time goes in v4:
time: 23.4 us; the launch traced here: 23.2 us
  Pallas kernels  20.5 us (88%)
  local copies, waits for them, and re-layouts  1.42 us (6%)
  between operations  1.29 us (6%)
    pallas_call x1, Pallas kernels, shards(): pl.pallas_call(functools.partial(kernel, tiles), out_shape=(pltpu.VMEM((N...  20.5 us
    unnamed x2, local copies, waits for them, and re-layouts  1.42 us

profile of v4, /device:TPU:0, one launch (start us, length us, event | category | flops | bytes accessed | tf_op | source)
XLA Modules:
  0.0 23.2 jit_solution(10599418880821536938)
XLA Ops:
  1.3 20.5 %shard_map.113 = (bf16[32,64,128]{2,1,0:T(8,128)(2,1)S(1)}, f32[2,2,32,128]{3,2,1,0:T(8,128)S(1)}) custom-call(f32[2,2,32,128]{3,2,1,0:T(8,128)} %now.1, f32[2,2,32,128]{3,2,1,0:T(8,128)} %prev_in.1, s32[2,32,128]{2,1,0:T(8,128)} %facies_in.1, f32[8]{0:T(128)} %vel_in.1, f32[8]{0:T(128)} %eps_in.1, f32[8]{0:T(128)} %tilt_in.1, s32[1]{0:T(128)S(6)} %copy.16.src_in, ...), custom_call_target="tpu_custom_call" | custom-call | tf_op jit(solution)/shard_map/pallas_call | solution.py:445
  21.8 0.8 %copy.14 = bf16[32,32,2,128]{3,2,1,0:T(2,128)(2,1)} copy(bf16[32,32,2,128]{3,2,1,0:T(2,128)(2,1)S(1)} %bitcast.2) | data formatting | bytes 1048576
  22.6 0.6 %copy.15 = f32[2,2,32,128]{3,2,1,0:T(8,128)} copy(f32[2,2,32,128]{3,2,1,0:T(8,128)S(1)} %get-tuple-element.7) | data formatting | bytes 131072
